TPU v7x, 256 devices: a whole 4x4x8 slice. The times are simulated.
256 devices in a mesh: grp: 2 (over core), dom: 64 (over y_lo, z, x), sub: 2 (over y_hi).
Axes of the slice: x: 4, y: 4 (y_hi: 2, y_lo: 2; y = y_hi * 2 + y_lo), z: 8, core: 2. Of those that a mesh axis runs over, the one named last changes fastest.
Arguments:
- positions: float32 [3, 65536], P(None, ('grp', 'dom', 'sub')), may hold values from 0 to 4
- charges: float32 [65536], P(('grp', 'dom', 'sub')), may hold values from -3 to 3
- polar: float32 [65536], P(('grp', 'dom', 'sub')), may hold values from 0.1 to 0.6
- features: bfloat16 [65536, 256], P(('grp', 'dom', 'sub')), may hold values from -6 to 6
- neighbours: int32 [65536, 32], P(('grp', 'dom', 'sub')), may hold values from 0 to 512, as said below
- send_rows: int32 [2, 32768], P(None, ('grp', 'dom', 'sub')), may hold values from 0 to 255
- blocks: int32 [1024], P(('grp', 'dom', 'sub')), may hold values from 0 to 255
- radial_in: bfloat16 [2, 8, 64], replicated, may hold values from -2 to 2
- radial_mid: bfloat16 [2, 2, 64, 64], replicated, may hold values from -0.75 to 0.75
- radial_out: bfloat16 [2, 64, 256], replicated, may hold values from -0.75 to 0.75
- node_in: bfloat16 [2, 256, 256], replicated, may hold values from -0.375 to 0.375
- node_out: bfloat16 [2, 256, 256], replicated, may hold values from -0.375 to 0.375
- field_gain: float32 [256], replicated, may hold values from -3 to 3
- readout: bfloat16 [256, 2], replicated, may hold values from -0.375 to 0.375
Outputs:
- site_result: float32 [3, 65536], P(None, ('grp', 'dom', 'sub'))
- response: float32 [3, 65536], P(None, ('grp', 'dom', 'sub'))
Inputs may be any that keep to these rules, and one draw needn't show every extreme that they name: `neighbours`: entries below 256 name the block's own sites, entries from 256 to 511 its lent sites, 512 an empty slot; empty slots follow the used ones. `blocks`: repeats may occur.
All inputs are finite; a program needn't handle non-finite values.
Results may differ from a plain program's by a relative error of at most 0.0022.
The roundings to bfloat16 on the way count: a program that leaves them out, or rounds other values in their place, can miss the bound.
Values may be sent and summed in bfloat16 or wider, within the bound.
No kernel may reach another device: no remote copies, remote signals or barrier semaphores. Data moves between devices by JAX's collectives and lax.ppermute only.
A program may use at most 64 MiB of HBM per device.

v0:
```python
import jax
import jax.numpy as jnp
from jax import lax
from jax.sharding import PartitionSpec as P

BASIS = 8
LAYERS = 2
SWEEPS = 4
BLOCK = 128
SMOOTH = 1.0
GAMMA = 1.0
SPACING = 0.75


def with_halo(block, sides, width):
    for axis, dim in sides:
        count = lax.axis_size(axis)
        forward = [(i, i + 1) for i in range(count - 1)]
        backward = [(target, source) for source, target in forward]
        low = lax.ppermute(
            lax.slice_in_dim(block, block.shape[dim] - width, None, axis=dim), axis, forward
        )
        high = lax.ppermute(lax.slice_in_dim(block, 0, width, axis=dim), axis, backward)
        block = jnp.concatenate([low, block, high], axis=dim)
    return block


def partner_2(value, axis, bit):
    mask = 2**bit
    pairs = [(source, source ^ mask) for source in range(lax.axis_size(axis))]
    return lax.ppermute(value, axis, pairs)


def field_at(target, source, charge, dipole):
    tile_count = target.shape[1] // BLOCK
    tiles = target.reshape(3, tile_count, BLOCK).transpose(1, 0, 2)

    def field_one_tile(target_tile):
        offset = target_tile[:, :, None] - source[:, None, :]
        dist_sq = jnp.sum(offset * offset, axis=0) + SMOOTH
        inverse = lax.rsqrt(dist_sq)
        inverse_cube = inverse * inverse * inverse
        inverse_fifth = inverse_cube * inverse * inverse
        projected = jnp.sum(offset * dipole[:, None, :], axis=0)
        source_scale = charge[None, :] * inverse_cube + 3.0 * projected * inverse_fifth
        return jnp.sum(
            offset * source_scale[None] - dipole[:, None, :] * inverse_cube[None], axis=2
        )

    return lax.map(field_one_tile, tiles).transpose(1, 0, 2).reshape(3, -1)


def slot_field(offset, dist_sq, source_charge, source_dipole):
    inverse = lax.rsqrt(dist_sq)
    inverse_cube = inverse * inverse * inverse
    inverse_fifth = inverse_cube * inverse * inverse
    projected = jnp.sum(offset * source_dipole, axis=0)
    source_scale = source_charge * inverse_cube + 3.0 * projected * inverse_fifth
    return jnp.sum(offset * source_scale[None] - source_dipole * inverse_cube[None], axis=1)


def message_update(
    hidden, lifted_table, radial_basis, slot_major, w_first, w_middle, w_last, w_node
):
    row_count, channel_count = hidden.shape
    slot_count = slot_major.shape[0]
    basis_width = radial_basis.shape[2]
    tile_count = row_count // BLOCK

    def message_one_tile(tile_index):
        start = tile_index * BLOCK
        basis_tile = lax.dynamic_slice_in_dim(radial_basis, start, BLOCK, 1).reshape(
            slot_count * BLOCK, basis_width
        )
        index_tile = lax.dynamic_slice_in_dim(slot_major, start, BLOCK, 1)
        first_hidden = jax.nn.silu(
            jnp.dot(basis_tile, w_first, preferred_element_type=jnp.float32)
        ).astype(jnp.bfloat16)
        second_hidden = jax.nn.silu(
            jnp.dot(first_hidden, w_middle[0], preferred_element_type=jnp.float32)
        ).astype(jnp.bfloat16)
        third_hidden = jax.nn.silu(
            jnp.dot(second_hidden, w_middle[1], preferred_element_type=jnp.float32)
        ).astype(jnp.bfloat16)
        edge_weight = jnp.dot(third_hidden, w_last, preferred_element_type=jnp.float32).reshape(
            slot_count, BLOCK, channel_count
        )
        source = lifted_table[index_tile].astype(jnp.float32)
        summed = jnp.sum(edge_weight * source, axis=0)
        return summed / slot_count

    message = (
        lax.map(message_one_tile, jnp.arange(tile_count, dtype=jnp.int32))
        .reshape(row_count, channel_count)
        .astype(jnp.bfloat16)
    )
    update = jax.nn.silu(jnp.dot(message, w_node, preferred_element_type=jnp.float32))
    return (hidden.astype(jnp.float32) + update).astype(jnp.bfloat16)


def extend_cols(values, rim_rows, rim_width):
    empty_entry = jnp.zeros(values.shape[:-1] + (1,), values.dtype)
    return jnp.concatenate(
        [values, rim_rows[..., :rim_width], rim_rows[..., 3 * rim_width :], empty_entry], axis=-1
    )


def extend_rows(values, rim_rows, rim_width):
    empty_entry = jnp.zeros((1,) + values.shape[1:], values.dtype)
    return jnp.concatenate(
        [values, rim_rows[:rim_width], rim_rows[3 * rim_width :], empty_entry], axis=0
    )


def local(
    positions,
    charges,
    polar,
    features,
    neighbours,
    send_rows,
    blocks,
    radial_in,
    radial_mid,
    radial_out,
    node_in,
    node_out,
    field_gain,
    readout,
):
    rim_width = send_rows.shape[1]
    row_count = positions.shape[1]
    block_width = BLOCK
    own_blocks = row_count // block_width
    listed_count = blocks.shape[0]
    domain_count = lax.axis_size(("dom", "sub"))
    domain_index = lax.axis_index(("dom", "sub"))
    group_blocks = own_blocks * domain_count
    learned = lax.axis_index("grp") == 0
    slot_major = neighbours.T
    local_data = jnp.concatenate([positions, charges[None], polar[None]], axis=0)
    outgoing = jnp.concatenate([local_data[:, send_rows[1]], local_data[:, send_rows[0]]], axis=1)
    rim_rows = with_halo(outgoing, ((("dom", "sub"), 1),), rim_width)
    site_table = extend_cols(local_data, rim_rows, rim_width)
    partner = partner_2(local_data, "grp", 0)
    others = lax.all_gather(partner, ("dom", "sub"), axis=1, tiled=True)
    near_sites = jnp.take(others.reshape(5, -1, block_width), blocks, axis=1).reshape(5, -1)
    outside = field_at(positions, near_sites[:3], near_sites[3], jnp.zeros_like(near_sites[:3]))
    offset = positions[:, None, :] - site_table[:3][:, slot_major]
    dist_sq = jnp.sum(offset * offset, axis=0) + SMOOTH
    strength = jnp.sqrt(1.0 + jnp.sum(outside * outside, axis=0))
    hidden = (features.astype(jnp.float32) + strength[:, None] * field_gain[None, :]).astype(
        jnp.bfloat16
    )
    centres = jnp.arange(BASIS, dtype=jnp.float32) * SPACING
    radial_basis = jnp.exp(-GAMMA * (jnp.sqrt(dist_sq)[:, :, None] - centres) ** 2).astype(
        jnp.bfloat16
    )
    for layer_index in range(LAYERS):
        lifted = lax.cond(
            learned,
            lambda h: jnp.dot(h, node_in[layer_index], preferred_element_type=jnp.float32).astype(
                jnp.bfloat16
            ),
            lambda h: jnp.zeros_like(h),
            hidden,
        )
        lent = jnp.concatenate([lifted[send_rows[1]], lifted[send_rows[0]]], axis=0)
        lifted_rims = with_halo(lent, ((("dom", "sub"), 0),), rim_width)
        lifted_table = extend_rows(lifted, lifted_rims, rim_width)
        hidden = lax.cond(
            learned,
            lambda h, t: message_update(
                h,
                t,
                radial_basis,
                slot_major,
                radial_in[layer_index],
                radial_mid[layer_index],
                radial_out[layer_index],
                node_out[layer_index],
            ),
            lambda h, t: h,
            hidden,
            lifted_table,
        )
    readouts = jnp.dot(hidden, readout, preferred_element_type=jnp.float32)
    charge = readouts[:, 0]
    energy = readouts[:, 1]
    fixed_field = outside + slot_field(
        offset, dist_sq, site_table[3][slot_major], jnp.zeros_like(offset)
    )
    dipole = jnp.where(learned, 0.0, polar[None] * fixed_field)
    for sweep_index in range(SWEEPS):
        lent_dipoles = jnp.concatenate([dipole[:, send_rows[1]], dipole[:, send_rows[0]]], axis=1)
        dipole_rims = with_halo(lent_dipoles, ((("dom", "sub"), 1),), rim_width)
        dipole_table = extend_cols(dipole, dipole_rims, rim_width)
        dipole = lax.cond(
            learned,
            lambda d, t: d,
            lambda d, t: polar[None]
            * (
                fixed_field + slot_field(offset, dist_sq, jnp.zeros_like(dist_sq), t[:, slot_major])
            ),
            dipole,
            dipole_table,
        )
    site_result = jnp.where(learned, jnp.stack([charge, energy, strength]), dipole)
    source_charge = jnp.where(learned, charge, 0.0)
    source_dipole = jnp.where(learned, 0.0, dipole)
    response_term = field_at(near_sites[:3], positions, source_charge, source_dipole)
    scattered = (
        jnp.zeros((3, group_blocks, block_width), jnp.float32)
        .at[:, blocks]
        .add(response_term.reshape(3, listed_count, block_width))
        .reshape(3, -1)
    )
    total = lax.psum(scattered, ("dom", "sub"))
    own_share = lax.dynamic_slice_in_dim(total, domain_index * row_count, row_count, 1)
    response = partner_2(own_share, "grp", 0)
    return (site_result, response)


def solution(mesh):
    in_specs = (
        P(None, ("grp", "dom", "sub")),
        P(("grp", "dom", "sub")),
        P(("grp", "dom", "sub")),
        P(("grp", "dom", "sub"), None),
        P(("grp", "dom", "sub"), None),
        P(None, ("grp", "dom", "sub")),
        P(("grp", "dom", "sub")),
        P(),
        P(),
        P(),
        P(),
        P(),
        P(),
        P(),
    )
    out_specs = (P(None, ("grp", "dom", "sub")), P(None, ("grp", "dom", "sub")))
    return jax.shard_map(local, mesh=mesh, in_specs=in_specs, out_specs=out_specs, check_vma=False)
```

profile of v0, /device:TPU:1, one launch (start us, length us, event | category | flops | bytes accessed | tf_op | source)
XLA Modules:
  0.0 878.2 jit_solution(3538958461297963734)
XLA Ops:
  14.7 5.5 collective-permute-start.1
  24.2 32.9 %gather_fusion.14 = f32[8192]{0:T(1024)S(1)} fusion(f32[513]{0:T(1024)S(1)} %slice_reduce_fusion, s32[8192]{0:T(1024)S(1)} %broadcast_clamp_fusion.4), kind=kCustom, calls=%fused_computation.14 | custom fusion | bytes 98304 | tf_op jit(solution)/shard_map/gather | solution.py:191
  57.2 27.9 %gather_fusion.9 = f32[8192,3]{1,0:T(8,128)} fusion(f32[3,513]{0,1:T(8,128)S(1)} %copy.124, s32[8192]{0:T(1024)S(1)} %broadcast_clamp_fusion.4), kind=kCustom, calls=%fused_computation.9 | custom fusion | bytes 229376 | tf_op jit(solution)/shard_map/gather | solution.py:149
  94.0 296.4 %all_gather.3 = f32[5,32768]{1,0:T(8,128)S(1)} all-gather(f32[5,256]{1,0:T(8,128)S(1)} %collective-permute-done), channel_id=1, replica_groups=mesh['grp'=2,'dom'=64,'sub'=2] {'dom','sub'}, dimensions={1}, use_global_device_ids=true | all-gather | bytes 660480 | tf_op jit(solution)/shard_map/all_gather | solution.py:146
  395.2 5.5 collective-permute-start.7
  402.1 36.6 %conditional.12 = (f32[3,256]{0,1:T(8,128)S(1)}) conditional(s32[]{:T(128)} %convert_element_type.76, (f32[256]{0:T(256)S(1)}, f32[32,256]{1,0:T(8,128)S(1)}, s32[32,256]{1,0:T(8,128)S(1)}, f32[3,513]{1,0:T(4,128)S(1)}, f32[3,32,256]{0,2,1:T(8,128)}, /*index=5*/f32[3,256]{0,1:T(8,128)S(1)}) %tuple.225, f32[3,256]{0,1:T(8,128)S(1)} %get-tuple-element.543), branch_computations={%region_23.26_spmd, %region_26.27_spmd} | conditional | flops 238336 | bytes 1860696 | solution.py:198
  402.3 27.9 %gather_fusion = f32[8192,3]{1,0:T(8,128)} fusion(f32[3,513]{0,1:T(8,128)S(1)} %copy.129, s32[8192]{0:T(1024)S(1)} %broadcast_clamp_fusion), kind=kCustom, calls=%fused_computation.2 | custom fusion | bytes 229376 | tf_op jit(solution)/shard_map/cond/branch_0_fun/gather | solution.py:203
  430.2 4.8 multiply_reduce_fusion
  441.3 6.1 collective-permute-start.9
  448.9 36.7 %conditional.13 = (f32[3,256]{0,1:T(8,128)S(1)}) conditional(s32[]{:T(128)} %convert_element_type.76, (f32[256]{0:T(256)S(1)}, f32[32,256]{1,0:T(8,128)S(1)}, s32[32,256]{1,0:T(8,128)S(1)}, f32[3,513]{1,0:T(4,128)S(1)}, f32[3,32,256]{0,2,1:T(8,128)}, /*index=5*/f32[3,256]{0,1:T(8,128)S(1)}) %tuple.226, f32[3,256]{0,1:T(8,128)S(1)} %get-tuple-element.898), branch_computations={%region_27.30_spmd, %region_30.31_spmd} | conditional | flops 238336 | bytes 1860696 | solution.py:198
  449.1 27.9 %gather_fusion.1 = f32[8192,3]{1,0:T(8,128)} fusion(f32[3,513]{0,1:T(8,128)S(1)} %copy.133, s32[8192]{0:T(1024)S(1)} %broadcast_clamp_fusion.1), kind=kCustom, calls=%fused_computation.3 | custom fusion | bytes 229376 | tf_op jit(solution)/shard_map/cond/branch_0_fun/gather | solution.py:203
  477.0 4.8 multiply_reduce_fusion.1
  488.1 6.4 collective-permute-start.11
  497.9 6.7 collective-permute-start.3
  504.9 36.6 %conditional.14 = (f32[3,256]{0,1:T(8,128)S(1)}) conditional(s32[]{:T(128)} %convert_element_type.76, (f32[256]{0:T(256)S(1)}, f32[32,256]{1,0:T(8,128)S(1)}, s32[32,256]{1,0:T(8,128)S(1)}, f32[3,513]{1,0:T(4,128)S(1)}, f32[3,32,256]{0,2,1:T(8,128)}, /*index=5*/f32[3,256]{0,1:T(8,128)S(1)}) %tuple.227, f32[3,256]{0,1:T(8,128)S(1)} %get-tuple-element.899), branch_computations={%region_31.34_spmd, %region_34.35_spmd} | conditional | flops 238336 | bytes 1860696 | solution.py:198
  505.1 27.9 %gather_fusion.2 = f32[8192,3]{1,0:T(8,128)} fusion(f32[3,513]{0,1:T(8,128)S(1)} %copy.137, s32[8192]{0:T(1024)S(1)} %broadcast_clamp_fusion.2), kind=kCustom, calls=%fused_computation.4 | custom fusion | bytes 229376 | tf_op jit(solution)/shard_map/cond/branch_0_fun/gather | solution.py:203
  533.0 4.8 multiply_reduce_fusion.2
  544.1 6.4 collective-permute-start.13
  555.2 6.4 collective-permute-start.5
  561.6 36.6 %conditional.15 = (f32[3,256]{0,1:T(8,128)S(1)}) conditional(s32[]{:T(128)} %convert_element_type.76, (f32[256]{0:T(256)S(1)}, f32[32,256]{1,0:T(8,128)S(1)}, s32[32,256]{1,0:T(8,128)S(1)}, f32[3,513]{1,0:T(4,128)S(1)}, f32[3,32,256]{0,2,1:T(8,128)}, /*index=5*/f32[3,256]{0,1:T(8,128)S(1)}) %tuple.228, f32[3,256]{0,1:T(8,128)S(1)} %get-tuple-element.900), branch_computations={%region_35.38_spmd, %region_38.39_spmd} | conditional | flops 238336 | bytes 1860696 | solution.py:198
  561.8 27.9 %gather_fusion.3 = f32[8192,3]{1,0:T(8,128)} fusion(f32[3,513]{0,1:T(8,128)S(1)} %copy.141, s32[8192]{0:T(1024)S(1)} %broadcast_clamp_fusion.3), kind=kCustom, calls=%fused_computation.5 | custom fusion | bytes 229376 | tf_op jit(solution)/shard_map/cond/branch_0_fun/gather | solution.py:203
  589.7 4.8 multiply_reduce_fusion.3
  602.6 261.5 %all-reduce.2.cloned.1.call-done = f32[3,32768]{1,0:T(4,128)} async-done(((f32[3,32768]{1,0:T(4,128)}), f32[3,32768]{1,0:T(4,128)}) %all-reduce.2.cloned.1.call-update) | async-done | bytes 393232 | tf_op jit(solution)/shard_map/psum | solution.py:218
  864.8 5.2 collective-permute-start.15
  (218 shorter events, 68.6 us)
Async XLA Ops:
  7.2 591.5 %copy-start = (bf16[256,2]{0,1:T(2,128)(2,1)S(1)}, bf16[256,2]{0,1:T(2,128)(2,1)}, u32[]{:S(2)}) copy-start(bf16[256,2]{0,1:T(2,128)(2,1)} %param.51) | copy-start | bytes 3076
  7.2 856.9 %all-reduce.2.cloned.1.call-start = ((), (), s32[]{:S(2)}) async-start(), calls=%async_computation | async-start | bytes 1048576 | tf_op jit(solution)/shard_map/psum | solution.py:218
  8.0 86.1 %collective-permute-start = (f32[5,256]{1,0:T(8,128)S(1)}, f32[5,256]{1,0:T(8,128)S(1)}, u32[]{:S(2)}, u32[]{:S(2)}) collective-permute-start(f32[5,256]{1,0:T(8,128)S(1)} %pad_maximum_fusion), channel_id=1, source_target_pairs={{0,128},{128,0},{1,129},{129,1},{2,130},{130,2},{3,131},{131,3},{4... | collective-permute-start | bytes 15368 | tf_op jit(solution)/shard_map/ppermute | solution.py:31
  12.8 10.5 %collective-permute-start.2 = (f32[5,128]{0,1:T(8,128)S(1)}, f32[5,128]{0,1:T(8,128)S(1)}, u32[]{:S(2)}, u32[]{:S(2)}) collective-permute-start(f32[5,128]{0,1:T(8,128)S(1)} %bitcast.260), channel_id=1, source_target_pairs={{1,0},{2,1},{3,2},{4,3},{5,4},{6,5},{7,6},{8,7},{9,8},{10,9},{11,1... | collective-permute-start | bytes 7688 | tf_op jit(solution)/shard_map/ppermute | solution.py:23
  14.7 8.6 collective-permute-start.1
  89.6 301.4 %copy-start.12 = (f32[3,256]{1,0:T(4,128)S(1)}, f32[3,256]{1,0:T(4,128)}, u32[]{:S(2)}) copy-start(f32[3,256]{1,0:T(4,128)} %param.38) | copy-start | bytes 9220
  393.9 6.9 collective-permute-start.8
  395.2 6.8 collective-permute-start.7
  440.0 7.5 collective-permute-start.10
  441.3 7.4 collective-permute-start.9
  448.8 45.7 %copy-start.14 = (bf16[256,256]{1,0:T(8,128)(2,1)S(1)}, bf16[256,256]{1,0:T(8,128)(2,1)}, u32[]{:S(2)}) copy-start(bf16[256,256]{1,0:T(8,128)(2,1)} %param.41) | copy-start | bytes 393220
  448.8 45.8 %copy-start.13 = (bf16[2,256,256]{2,1,0:T(8,128)(2,1)S(1)}, bf16[2,256,256]{2,1,0:T(8,128)(2,1)}, u32[]{:S(2)}) copy-start(bf16[2,256,256]{2,1,0:T(8,128)(2,1)} %param.48) | copy-start | bytes 786436
  486.8 17.9 %collective-permute-start.12 = (f32[3,128]{0,1:T(8,128)S(1)}, f32[3,128]{0,1:T(8,128)S(1)}, u32[]{:S(2)}, u32[]{:S(2)}) collective-permute-start(f32[3,128]{0,1:T(8,128)S(1)} %bitcast.263), channel_id=1, source_target_pairs={{1,0},{2,1},{3,2},{4,3},{5,4},{6,5},{7,6},{8,7},{9,8},{10,9},{11,1... | collective-permute-start | bytes 4616 | tf_op jit(solution)/shard_map/ppermute | solution.py:23
  488.1 16.7 %collective-permute-start.11 = (f32[3,128]{0,1:T(8,128)S(1)}, f32[3,128]{0,1:T(8,128)S(1)}, u32[]{:S(2)}, u32[]{:S(2)}) collective-permute-start(f32[3,128]{0,1:T(8,128)S(1)} %bitcast.262), channel_id=1, source_target_pairs={{0,1},{1,2},{2,3},{3,4},{4,5},{5,6},{6,7},{7,8},{8,9},{9,10},{10,1... | collective-permute-start | bytes 4616 | tf_op jit(solution)/shard_map/ppermute | solution.py:20
  496.6 55.3 %collective-permute-start.4 = (bf16[128,256]{1,0:T(8,128)(2,1)S(1)}, bf16[128,256]{1,0:T(8,128)(2,1)S(1)}, u32[]{:S(2)}, u32[]{:S(2)}) collective-permute-start(bf16[128,256]{1,0:T(8,128)(2,1)S(1)} %gather_fusion.11), channel_id=1, source_target_pairs={{1,0},{2,1},{3,2},{4,3},{5,4},{6,5},{7,6},{8,7},{9,8},{10,9},{11,1... | collective-permute-start | bytes 196616 | tf_op jit(solution)/shard_map/ppermute | solution.py:23
  497.9 54.0 %collective-permute-start.3 = (bf16[128,256]{1,0:T(8,128)(2,1)S(1)}, bf16[128,256]{1,0:T(8,128)(2,1)S(1)}, u32[]{:S(2)}, u32[]{:S(2)}) collective-permute-start(bf16[128,256]{1,0:T(8,128)(2,1)S(1)} %gather_fusion.10), channel_id=1, source_target_pairs={{0,1},{1,2},{2,3},{3,4},{4,5},{5,6},{6,7},{7,8},{8,9},{9,10},{10,1... | collective-permute-start | bytes 196616 | tf_op jit(solution)/shard_map/ppermute | solution.py:20
  504.9 47.2 %copy-start.15 = (bf16[2,2,64,64]{3,2,1,0:T(8,128)(2,1)S(1)}, bf16[2,2,64,64]{3,2,1,0:T(8,128)(2,1)}, u32[]{:S(2)}) copy-start(bf16[2,2,64,64]{3,2,1,0:T(8,128)(2,1)} %param.46) | copy-start | bytes 98308
  504.9 47.2 %copy-start.16 = (bf16[2,64,256]{2,1,0:T(8,128)(2,1)S(1)}, bf16[2,64,256]{2,1,0:T(8,128)(2,1)}, u32[]{:S(2)}) copy-start(bf16[2,64,256]{2,1,0:T(8,128)(2,1)} %param.47) | copy-start | bytes 196612
  504.9 47.2 %copy-start.19 = (bf16[2,8,64]{2,1,0:T(8,128)(2,1)S(1)}, bf16[2,8,64]{2,1,0:T(8,128)(2,1)}, u32[]{:S(2)}) copy-start(bf16[2,8,64]{2,1,0:T(8,128)(2,1)} %param.45) | copy-start | bytes 6148
  542.8 7.9 collective-permute-start.14
  544.1 7.7 collective-permute-start.13
  553.9 44.4 %collective-permute-start.6 = (bf16[128,256]{1,0:T(8,128)(2,1)S(1)}, bf16[128,256]{1,0:T(8,128)(2,1)S(1)}, u32[]{:S(2)}, u32[]{:S(2)}) collective-permute-start(bf16[128,256]{1,0:T(8,128)(2,1)S(1)} %gather_fusion.13), channel_id=1, source_target_pairs={{1,0},{2,1},{3,2},{4,3},{5,4},{6,5},{7,6},{8,7},{9,8},{10,9},{11,1... | collective-permute-start | bytes 196616 | tf_op jit(solution)/shard_map/ppermute | solution.py:23
  555.2 43.1 %collective-permute-start.5 = (bf16[128,256]{1,0:T(8,128)(2,1)S(1)}, bf16[128,256]{1,0:T(8,128)(2,1)S(1)}, u32[]{:S(2)}, u32[]{:S(2)}) collective-permute-start(bf16[128,256]{1,0:T(8,128)(2,1)S(1)} %gather_fusion.12), channel_id=1, source_target_pairs={{0,1},{1,2},{2,3},{3,4},{4,5},{5,6},{6,7},{7,8},{8,9},{9,10},{10,1... | collective-permute-start | bytes 196616 | tf_op jit(solution)/shard_map/ppermute | solution.py:20
  864.8 6.0 collective-permute-start.15
  (16 other events, 109.3 us)
Sparse Core Ops, SparseCore 0:
  602.7 261.3 all-reduce.1
where the time goes:
time: 879 us; the launch traced here: 878 us
  blocking collectives  296 us (34%)
  waiting for transfers between devices  265 us (30%)
  local copies, waits for them, and re-layouts  195 us (22%)
  starting transfers between devices  60.5 us (7%)
  other arithmetic  45.1 us (5%)
  between operations  14.8 us (2%)
    all_gather x1, blocking collectives, local(): others = lax.all_gather(partner, ('dom', 'sub'), axis=1, tiled=True)  296 us
    psum x1, waiting for transfers between devices, local(): total = lax.psum(scattered, ('dom', 'sub'))  262 us
    gather x4, local copies, waits for them, and re-layouts, local(): t[:, slot_major]  112 us
    ppermute x7, starting transfers between devices, with_halo(): lax.ppermute(lax.slice_in_dim(block, block.shape[dim] - width, None, axis...  43 us
    gather x2, local copies, waits for them, and re-layouts, local(): site_table[3][slot_major]  32.9 us
    gather x1, local copies, waits for them, and re-layouts, local(): offset = positions[:, None, :] - site_table[:3][:, slot_major]  27.9 us
    reduce_sum x5, other arithmetic, slot_field(): projected = jnp.sum(offset * source_dipole, axis=0)  23.5 us
  transfers between devices with their start and end apart: 17, of which 5 were waited for; matrix products, arithmetic and copies ran while one was open for 17% of the time, Pallas kernels for 0%

commit v1 on v0

--- a/solution.py
+++ b/solution.py
@@ -215,7 +215,9 @@
         .add(response_term.reshape(3, listed_count, block_width))
         .reshape(3, -1)
     )
-    total = lax.psum(scattered, ("dom", "sub"))
+    total = scattered
+    for mesh_axis in ("dom", "sub"):
+        total = lax.psum(total, mesh_axis)
     own_share = lax.dynamic_slice_in_dim(total, domain_index * row_count, row_count, 1)
     response = partner_2(own_share, "grp", 0)
     return (site_result, response)

time: 879 us -> 1310 us (1.49)
  waiting for transfers between devices: 265 us -> 696 us
    psum x1 -> x2, waiting for transfers between devices: 262 us -> 692 us  [local(): total = lax.psum(total, mesh_axis)]
  transfers between devices with their start and end apart: 17 -> 18, of which waited for: 5 -> 6; matrix products, arithmetic and copies ran while one was open for 17% -> 11% of each run, Pallas kernels for 0% -> 0%
where the time goes in v1:
time: 1310 us; the launch traced here: 1300 us
  waiting for transfers between devices  696 us (53%)
  blocking collectives  296 us (23%)
  local copies, waits for them, and re-layouts  195 us (15%)
  starting transfers between devices  56 us (4%)
  other arithmetic  45.1 us (3%)
  between operations  14.8 us (1%)
    psum x2, waiting for transfers between devices, local(): total = lax.psum(total, mesh_axis)  692 us
    all_gather x1, blocking collectives, local(): others = lax.all_gather(partner, ('dom', 'sub'), axis=1, tiled=True)  296 us
    gather x4, local copies, waits for them, and re-layouts, local(): t[:, slot_major]  112 us
    ppermute x7, starting transfers between devices, with_halo(): lax.ppermute(lax.slice_in_dim(block, block.shape[dim] - width, None, axis...  43 us
    gather x2, local copies, waits for them, and re-layouts, local(): site_table[3][slot_major]  32.9 us
    gather x1, local copies, waits for them, and re-layouts, local(): offset = positions[:, None, :] - site_table[:3][:, slot_major]  27.9 us
  transfers between devices with their start and end apart: 18, of which 6 were waited for; matrix products, arithmetic and copies ran while one was open for 11% of the time, Pallas kernels for 0%

profile of v1, /device:TPU:1, one launch (start us, length us, event | category | flops | bytes accessed | tf_op | source)
XLA Modules:
  0.0 1304.6 jit_solution(12670022668591293518)
XLA Ops:
  14.7 5.5 collective-permute-start.1
  24.2 32.9 %gather_fusion.14 = f32[8192]{0:T(1024)S(1)} fusion(f32[513]{0:T(1024)S(1)} %slice_reduce_fusion, s32[8192]{0:T(1024)S(1)} %broadcast_clamp_fusion.4), kind=kCustom, calls=%fused_computation.14 | custom fusion | bytes 98304 | tf_op jit(solution)/shard_map/gather | solution.py:191
  57.2 27.9 %gather_fusion.9 = f32[8192,3]{1,0:T(8,128)} fusion(f32[3,513]{0,1:T(8,128)S(1)} %copy.124, s32[8192]{0:T(1024)S(1)} %broadcast_clamp_fusion.4), kind=kCustom, calls=%fused_computation.9 | custom fusion | bytes 229376 | tf_op jit(solution)/shard_map/gather | solution.py:149
  94.0 296.4 %all_gather.3 = f32[5,32768]{1,0:T(8,128)S(1)} all-gather(f32[5,256]{1,0:T(8,128)S(1)} %collective-permute-done), channel_id=1, replica_groups=mesh['grp'=2,'dom'=64,'sub'=2] {'dom','sub'}, dimensions={1}, use_global_device_ids=true | all-gather | bytes 660480 | tf_op jit(solution)/shard_map/all_gather | solution.py:146
  395.2 5.5 collective-permute-start.7
  402.1 36.6 %conditional.12 = (f32[3,256]{0,1:T(8,128)S(1)}) conditional(s32[]{:T(128)} %convert_element_type.76, (f32[256]{0:T(256)S(1)}, f32[32,256]{1,0:T(8,128)S(1)}, s32[32,256]{1,0:T(8,128)S(1)}, f32[3,513]{1,0:T(4,128)S(1)}, f32[3,32,256]{0,2,1:T(8,128)}, /*index=5*/f32[3,256]{0,1:T(8,128)S(1)}) %tuple.227, f32[3,256]{0,1:T(8,128)S(1)} %get-tuple-element.543), branch_computations={%region_23.26_spmd, %region_26.27_spmd} | conditional | flops 238336 | bytes 1860696 | solution.py:198
  402.3 27.9 %gather_fusion = f32[8192,3]{1,0:T(8,128)} fusion(f32[3,513]{0,1:T(8,128)S(1)} %copy.129, s32[8192]{0:T(1024)S(1)} %broadcast_clamp_fusion), kind=kCustom, calls=%fused_computation.2 | custom fusion | bytes 229376 | tf_op jit(solution)/shard_map/cond/branch_0_fun/gather | solution.py:203
  430.2 4.8 multiply_reduce_fusion
  441.3 6.1 collective-permute-start.9
  448.9 36.7 %conditional.13 = (f32[3,256]{0,1:T(8,128)S(1)}) conditional(s32[]{:T(128)} %convert_element_type.76, (f32[256]{0:T(256)S(1)}, f32[32,256]{1,0:T(8,128)S(1)}, s32[32,256]{1,0:T(8,128)S(1)}, f32[3,513]{1,0:T(4,128)S(1)}, f32[3,32,256]{0,2,1:T(8,128)}, /*index=5*/f32[3,256]{0,1:T(8,128)S(1)}) %tuple.228, f32[3,256]{0,1:T(8,128)S(1)} %get-tuple-element.898), branch_computations={%region_27.30_spmd, %region_30.31_spmd} | conditional | flops 238336 | bytes 1860696 | solution.py:198
  449.1 27.9 %gather_fusion.1 = f32[8192,3]{1,0:T(8,128)} fusion(f32[3,513]{0,1:T(8,128)S(1)} %copy.133, s32[8192]{0:T(1024)S(1)} %broadcast_clamp_fusion.1), kind=kCustom, calls=%fused_computation.3 | custom fusion | bytes 229376 | tf_op jit(solution)/shard_map/cond/branch_0_fun/gather | solution.py:203
  477.0 4.8 multiply_reduce_fusion.1
  488.1 6.4 collective-permute-start.11
  497.9 6.7 collective-permute-start.3
  504.9 36.6 %conditional.14 = (f32[3,256]{0,1:T(8,128)S(1)}) conditional(s32[]{:T(128)} %convert_element_type.76, (f32[256]{0:T(256)S(1)}, f32[32,256]{1,0:T(8,128)S(1)}, s32[32,256]{1,0:T(8,128)S(1)}, f32[3,513]{1,0:T(4,128)S(1)}, f32[3,32,256]{0,2,1:T(8,128)}, /*index=5*/f32[3,256]{0,1:T(8,128)S(1)}) %tuple.229, f32[3,256]{0,1:T(8,128)S(1)} %get-tuple-element.899), branch_computations={%region_31.34_spmd, %region_34.35_spmd} | conditional | flops 238336 | bytes 1860696 | solution.py:198
  505.1 27.9 %gather_fusion.2 = f32[8192,3]{1,0:T(8,128)} fusion(f32[3,513]{0,1:T(8,128)S(1)} %copy.137, s32[8192]{0:T(1024)S(1)} %broadcast_clamp_fusion.2), kind=kCustom, calls=%fused_computation.4 | custom fusion | bytes 229376 | tf_op jit(solution)/shard_map/cond/branch_0_fun/gather | solution.py:203
  533.0 4.8 multiply_reduce_fusion.2
  544.1 6.4 collective-permute-start.13
  555.2 6.4 collective-permute-start.5
  561.6 36.6 %conditional.15 = (f32[3,256]{0,1:T(8,128)S(1)}) conditional(s32[]{:T(128)} %convert_element_type.76, (f32[256]{0:T(256)S(1)}, f32[32,256]{1,0:T(8,128)S(1)}, s32[32,256]{1,0:T(8,128)S(1)}, f32[3,513]{1,0:T(4,128)S(1)}, f32[3,32,256]{0,2,1:T(8,128)}, /*index=5*/f32[3,256]{0,1:T(8,128)S(1)}) %tuple.230, f32[3,256]{0,1:T(8,128)S(1)} %get-tuple-element.900), branch_computations={%region_35.38_spmd, %region_38.39_spmd} | conditional | flops 238336 | bytes 1860696 | solution.py:198
  561.8 27.9 %gather_fusion.3 = f32[8192,3]{1,0:T(8,128)} fusion(f32[3,513]{0,1:T(8,128)S(1)} %copy.141, s32[8192]{0:T(1024)S(1)} %broadcast_clamp_fusion.3), kind=kCustom, calls=%fused_computation.5 | custom fusion | bytes 229376 | tf_op jit(solution)/shard_map/cond/branch_0_fun/gather | solution.py:203
  589.7 4.8 multiply_reduce_fusion.3
  602.6 607.4 %all-reduce.3.cloned.1.call-done = f32[3,32768]{1,0:T(4,128)} async-done(((f32[3,32768]{1,0:T(4,128)}), f32[3,32768]{1,0:T(4,128)}) %all-reduce.3.cloned.1.call-update) | async-done | bytes 393232 | tf_op jit(solution)/shard_map/psum | solution.py:220
  1210.0 85.0 %all-reduce.5.cloned.1.call-done = f32[3,32768]{1,0:T(4,128)} async-done(((f32[3,32768]{1,0:T(4,128)}), f32[3,32768]{1,0:T(4,128)}) %all-reduce.5.cloned.1.call-update) | async-done | bytes 393232 | tf_op jit(solution)/shard_map/psum | solution.py:220
  (221 shorter events, 69.4 us)
Async XLA Ops:
  7.2 591.5 %copy-start = (bf16[256,2]{0,1:T(2,128)(2,1)S(1)}, bf16[256,2]{0,1:T(2,128)(2,1)}, u32[]{:S(2)}) copy-start(bf16[256,2]{0,1:T(2,128)(2,1)} %param.51) | copy-start | bytes 3076
  7.2 1202.8 %all-reduce.3.cloned.1.call-start = ((), (), s32[]{:S(2)}) async-start(), calls=%async_computation | async-start | bytes 1048576 | tf_op jit(solution)/shard_map/psum | solution.py:220
  8.0 86.1 %collective-permute-start = (f32[5,256]{1,0:T(8,128)S(1)}, f32[5,256]{1,0:T(8,128)S(1)}, u32[]{:S(2)}, u32[]{:S(2)}) collective-permute-start(f32[5,256]{1,0:T(8,128)S(1)} %pad_maximum_fusion), channel_id=1, source_target_pairs={{0,128},{128,0},{1,129},{129,1},{2,130},{130,2},{3,131},{131,3},{4... | collective-permute-start | bytes 15368 | tf_op jit(solution)/shard_map/ppermute | solution.py:31
  12.8 10.5 collective-permute-start.2
  14.7 8.6 collective-permute-start.1
  89.6 301.4 %copy-start.12 = (f32[3,256]{1,0:T(4,128)S(1)}, f32[3,256]{1,0:T(4,128)}, u32[]{:S(2)}) copy-start(f32[3,256]{1,0:T(4,128)} %param.38) | copy-start | bytes 9220
  393.9 6.9 collective-permute-start.8
  395.2 6.8 collective-permute-start.7
  440.0 7.5 collective-permute-start.10
  441.3 7.4 collective-permute-start.9
  448.8 45.8 %copy-start.13 = (bf16[2,256,256]{2,1,0:T(8,128)(2,1)S(1)}, bf16[2,256,256]{2,1,0:T(8,128)(2,1)}, u32[]{:S(2)}) copy-start(bf16[2,256,256]{2,1,0:T(8,128)(2,1)} %param.48) | copy-start | bytes 786436
  486.8 17.9 %collective-permute-start.12 = (f32[3,128]{0,1:T(8,128)S(1)}, f32[3,128]{0,1:T(8,128)S(1)}, u32[]{:S(2)}, u32[]{:S(2)}) collective-permute-start(f32[3,128]{0,1:T(8,128)S(1)} %bitcast.263), channel_id=1, source_target_pairs={{1,0},{2,1},{3,2},{4,3},{5,4},{6,5},{7,6},{8,7},{9,8},{10,9},{11,1... | collective-permute-start | bytes 4616 | tf_op jit(solution)/shard_map/ppermute | solution.py:23
  488.1 16.7 %collective-permute-start.11 = (f32[3,128]{0,1:T(8,128)S(1)}, f32[3,128]{0,1:T(8,128)S(1)}, u32[]{:S(2)}, u32[]{:S(2)}) collective-permute-start(f32[3,128]{0,1:T(8,128)S(1)} %bitcast.262), channel_id=1, source_target_pairs={{0,1},{1,2},{2,3},{3,4},{4,5},{5,6},{6,7},{7,8},{8,9},{9,10},{10,1... | collective-permute-start | bytes 4616 | tf_op jit(solution)/shard_map/ppermute | solution.py:20
  496.6 55.3 %collective-permute-start.4 = (bf16[128,256]{1,0:T(8,128)(2,1)S(1)}, bf16[128,256]{1,0:T(8,128)(2,1)S(1)}, u32[]{:S(2)}, u32[]{:S(2)}) collective-permute-start(bf16[128,256]{1,0:T(8,128)(2,1)S(1)} %gather_fusion.11), channel_id=1, source_target_pairs={{1,0},{2,1},{3,2},{4,3},{5,4},{6,5},{7,6},{8,7},{9,8},{10,9},{11,1... | collective-permute-start | bytes 196616 | tf_op jit(solution)/shard_map/ppermute | solution.py:23
  497.9 54.0 %collective-permute-start.3 = (bf16[128,256]{1,0:T(8,128)(2,1)S(1)}, bf16[128,256]{1,0:T(8,128)(2,1)S(1)}, u32[]{:S(2)}, u32[]{:S(2)}) collective-permute-start(bf16[128,256]{1,0:T(8,128)(2,1)S(1)} %gather_fusion.10), channel_id=1, source_target_pairs={{0,1},{1,2},{2,3},{3,4},{4,5},{5,6},{6,7},{7,8},{8,9},{9,10},{10,1... | collective-permute-start | bytes 196616 | tf_op jit(solution)/shard_map/ppermute | solution.py:20
  504.9 47.2 %copy-start.15 = (bf16[2,2,64,64]{3,2,1,0:T(8,128)(2,1)S(1)}, bf16[2,2,64,64]{3,2,1,0:T(8,128)(2,1)}, u32[]{:S(2)}) copy-start(bf16[2,2,64,64]{3,2,1,0:T(8,128)(2,1)} %param.46) | copy-start | bytes 98308
  504.9 47.2 %copy-start.16 = (bf16[2,64,256]{2,1,0:T(8,128)(2,1)S(1)}, bf16[2,64,256]{2,1,0:T(8,128)(2,1)}, u32[]{:S(2)}) copy-start(bf16[2,64,256]{2,1,0:T(8,128)(2,1)} %param.47) | copy-start | bytes 196612
  504.9 47.2 %copy-start.19 = (bf16[2,8,64]{2,1,0:T(8,128)(2,1)S(1)}, bf16[2,8,64]{2,1,0:T(8,128)(2,1)}, u32[]{:S(2)}) copy-start(bf16[2,8,64]{2,1,0:T(8,128)(2,1)} %param.45) | copy-start | bytes 6148
  542.8 7.9 collective-permute-start.14
  544.1 7.7 collective-permute-start.13
  553.9 44.4 %collective-permute-start.6 = (bf16[128,256]{1,0:T(8,128)(2,1)S(1)}, bf16[128,256]{1,0:T(8,128)(2,1)S(1)}, u32[]{:S(2)}, u32[]{:S(2)}) collective-permute-start(bf16[128,256]{1,0:T(8,128)(2,1)S(1)} %gather_fusion.13), channel_id=1, source_target_pairs={{1,0},{2,1},{3,2},{4,3},{5,4},{6,5},{7,6},{8,7},{9,8},{10,9},{11,1... | collective-permute-start | bytes 196616 | tf_op jit(solution)/shard_map/ppermute | solution.py:23
  555.2 43.1 %collective-permute-start.5 = (bf16[128,256]{1,0:T(8,128)(2,1)S(1)}, bf16[128,256]{1,0:T(8,128)(2,1)S(1)}, u32[]{:S(2)}, u32[]{:S(2)}) collective-permute-start(bf16[128,256]{1,0:T(8,128)(2,1)S(1)} %gather_fusion.12), channel_id=1, source_target_pairs={{0,1},{1,2},{2,3},{3,4},{4,5},{5,6},{6,7},{7,8},{8,9},{9,10},{10,1... | collective-permute-start | bytes 196616 | tf_op jit(solution)/shard_map/ppermute | solution.py:20
  602.5 692.5 %all-reduce.5.cloned.1.call-start = ((), (), s32[]{:S(2)}) async-start(), calls=%async_computation.1 | async-start | bytes 1048576 | tf_op jit(solution)/shard_map/psum | solution.py:220
  1295.7 1.5 collective-permute-start.15
  (17 other events, 155.0 us)
Sparse Core Ops, SparseCore 0:
  602.7 607.2 all-reduce.2
  1212.8 82.1 all-reduce.4
